TPU v7x, 512 devices: a whole 4x8x8 slice. The times are simulated.
512 devices in a mesh: gx: 8 (over z_hi, core), gy: 8 (over y), gz: 8 (over x, z_lo).
Axes of the slice: x: 4, y: 8, z: 8 (z_hi: 4, z_lo: 2; z = z_hi * 2 + z_lo), core: 2. Of those that a mesh axis runs over, the one named last changes fastest.
Arguments:
- features: bfloat16 [8, 8, 8, 128, 128], P('gx', 'gy', 'gz'), may hold values from -6 to 6
- positions: float32 [8, 8, 8, 3, 128], P('gx', 'gy', 'gz'), may hold values from 0 to 1
- counts: int32 [8, 8, 8], P('gx', 'gy', 'gz'), may hold values from 1 to 128, as said below
- w_proj: bfloat16 [4, 128, 128], replicated, may hold values from -0.5 to 0.5
- w_mix: bfloat16 [128, 128], replicated, may hold values from -0.5 to 0.5
- w_long: bfloat16 [64, 128], replicated, may hold values from -0.75 to 0.75
- w_charge: bfloat16 [64, 128], replicated, may hold values from -0.5 to 0.5
- charge_bias: float32 [64], replicated, may hold values from -4 to 4
- w_energy: float32 [128], replicated, may hold values from -0.5 to 0.5
- k_filter: float32 [64, 2048], replicated, may hold values from 0.1 to 1
- k_index: int32 [3, 2048], replicated, may hold values from -6 to 6
Outputs:
- updated: bfloat16 [8, 8, 8, 128, 128], P('gx', 'gy', 'gz')
- energies: float32 [8, 8, 8, 128], P('gx', 'gy', 'gz')
- forces: float32 [8, 8, 8, 3, 128], P('gx', 'gy', 'gz')
Inputs may be any that keep to these rules, and one draw needn't show every extreme that they name: Slots 0 to counts[x,y,z] - 1 of cell (x,y,z) hold live atoms, the rest are padding; some cell holds 128 live atoms.
All inputs are finite; a program needn't handle non-finite values.
Results may differ from a plain program's by a relative error of at most 0.0068.
Values may be sent and summed in bfloat16 or wider, within the bound.
A program may use at most 64 MiB of HBM per device.

v0:
```python
import math
import jax
import jax.numpy as jnp
from jax import lax
from jax.sharding import PartitionSpec as P

CUTOFF = 0.9
GAMMAS = (1.0, 3.0, 8.0, 20.0)
PRECISE = lax.Precision.HIGHEST
CONTRACT_LAST = (((1,), (1,)), ((), ()))
CONTRACT_FIRST = (((0,), (0,)), ((), ()))


def extended(value, sides, width):
    for axis, dim in sides:
        peers, length = (lax.axis_size(axis), value.shape[dim])
        up = [(i, (i + 1) % peers) for i in range(peers)]
        down = [(j, i) for i, j in up]
        last = lax.slice_in_dim(value, length - width, length, axis=dim)
        initial = lax.slice_in_dim(value, 0, width, axis=dim)
        before = lax.ppermute(last, axis, up)
        after = lax.ppermute(initial, axis, down)
        value = jnp.concatenate([before, value, after], axis=dim)
    return value


def silu_grad(values):
    sigma = jax.nn.sigmoid(values)
    return sigma * (1.0 + values * (1.0 - sigma))


def pair_geometry(centre, others, neighbour):
    cell_shift = (
        jnp.stack([neighbour // 9, neighbour // 3 % 3, neighbour % 3]).astype(jnp.float32) - 1.0
    )
    offset_vec = others[:, None, :] + cell_shift[:, None, None] - centre[:, :, None]
    scaled = jnp.sum(offset_vec * offset_vec, axis=0) / (CUTOFF * CUTOFF)
    atom_count = centre.shape[1]
    slot_ids = jnp.arange(atom_count, dtype=jnp.int32)
    self_pair = (slot_ids[:, None] == slot_ids[None, :]) & (neighbour == 13)
    keep_mask = jnp.where(self_pair, 0.0, 1.0).astype(jnp.float32)
    envelope_base = jnp.maximum(1.0 - scaled, 0.0)
    decay_rates = jnp.asarray(GAMMAS, dtype=jnp.float32)[None, :, None]
    decay_terms = jnp.exp(-decay_rates * scaled[:, None, :]) * keep_mask[:, None, :]
    envelope = (envelope_base * envelope_base)[:, None, :]
    radial = decay_terms * envelope
    radial_slope = decay_terms * (-decay_rates * envelope - 2.0 * envelope_base[:, None, :])
    return (offset_vec, radial, radial_slope)


def phases(absolute, wave_vec, first_wave, wave_block):
    wave_part = wave_vec[:, first_wave : first_wave + wave_block]
    phase_angle = (
        absolute[0][:, None] * wave_part[0][None, :]
        + absolute[1][:, None] * wave_part[1][None, :]
        + absolute[2][:, None] * wave_part[2][None, :]
    )
    return (jnp.cos(phase_angle), jnp.sin(phase_angle))


def structure(weights_rows, absolute, wave_vec, wave_block):
    cosine_parts = []
    sine_parts = []
    for first_wave in range(0, wave_vec.shape[1], wave_block):
        cosine, sine_part = phases(absolute, wave_vec, first_wave, wave_block)
        cosine_parts.append(jnp.dot(weights_rows, cosine, precision=PRECISE))
        sine_parts.append(jnp.dot(weights_rows, sine_part, precision=PRECISE))
    return (jnp.concatenate(cosine_parts, axis=1), jnp.concatenate(sine_parts, axis=1))


def shards(
    features,
    positions,
    counts,
    w_proj,
    w_mix,
    w_long,
    w_charge,
    charge_bias,
    w_energy,
    k_filter,
    k_index,
):
    own_rows = features[0, 0, 0]
    centre = positions[0, 0, 0]
    atom_count, channels = own_rows.shape
    basis_count = w_proj.shape[0]
    waves = k_index.shape[1]
    wave_block = min(512, waves)
    grid_sizes = (lax.axis_size("gx"), lax.axis_size("gy"), lax.axis_size("gz"))
    scale_long = 4.0 / math.sqrt(atom_count * grid_sizes[0] * grid_sizes[1] * grid_sizes[2] * waves)
    cell_anchor = jnp.stack(
        [lax.axis_index("gx"), lax.axis_index("gy"), lax.axis_index("gz")]
    ).astype(jnp.float32)
    living = (jnp.arange(atom_count, dtype=jnp.int32) < counts[0, 0, 0]).astype(jnp.float32)
    masked = own_rows * living[:, None].astype(jnp.bfloat16)
    extent = jnp.asarray(grid_sizes, dtype=jnp.float32)
    wave_vec = 2.0 * math.pi * k_index.astype(jnp.float32) / extent[:, None]
    absolute = centre + cell_anchor[:, None]
    charges = (
        jax.nn.silu(
            lax.dot_general(w_charge, masked, CONTRACT_LAST, preferred_element_type=jnp.float32)
            + charge_bias[:, None]
        )
        * living[None, :]
    )
    stacked_rows = jnp.concatenate([charges, living[None, :]], axis=0)
    local_c, local_s = structure(stacked_rows, absolute, wave_vec, wave_block)
    totals = lax.psum(
        (local_c, local_s, jnp.sum(charges, axis=1), jnp.sum(living)), ("gx", "gy", "gz")
    )
    charge_mean = totals[2] / totals[3]
    neutral = (charges - charge_mean[:, None]) * living[None, :]
    row_count = charges.shape[0]
    struct_c = totals[0][:row_count] - charge_mean[:, None] * totals[0][row_count:]
    struct_s = totals[1][:row_count] - charge_mean[:, None] * totals[1][row_count:]
    near_pos = extended(positions, (("gx", 0), ("gy", 1), ("gz", 2)), 1).reshape(27, 3, atom_count)
    local_proj = jnp.einsum(
        "jc,bcd->bjd", masked, w_proj, preferred_element_type=jnp.float32
    ).astype(jnp.bfloat16)
    near_feat = extended(masked[None, None, None], (("gx", 0), ("gy", 1), ("gz", 2)), 1).reshape(
        27, atom_count, channels
    )

    def fetch_basis(neighbour):
        near_rows = lax.dynamic_index_in_dim(near_feat, neighbour, 0, keepdims=False)
        return (
            jnp.einsum("jc,bcd->bjd", near_rows, w_proj, preferred_element_type=jnp.float32)
            .astype(jnp.bfloat16)
            .reshape(basis_count * atom_count, channels)
        )

    def add_message(neighbour, message):
        others = lax.dynamic_index_in_dim(near_pos, neighbour, 0, keepdims=False)
        offset_vec, radial, radial_slope = pair_geometry(centre, others, neighbour)
        return message + jnp.dot(
            radial.astype(jnp.bfloat16).reshape(atom_count, -1),
            fetch_basis(neighbour),
            preferred_element_type=jnp.float32,
        )

    message = lax.fori_loop(0, 27, add_message, jnp.zeros((atom_count, channels), jnp.float32))
    filtered_cos = k_filter * struct_c
    filtered_sin = k_filter * struct_s
    potential = jnp.zeros(charges.shape, jnp.float32)
    for first_wave in range(0, waves, wave_block):
        cosine, sine_part = phases(absolute, wave_vec, first_wave, wave_block)
        potential = (
            potential
            + lax.dot_general(
                filtered_cos[:, first_wave : first_wave + wave_block],
                cosine,
                CONTRACT_LAST,
                precision=PRECISE,
            )
            + lax.dot_general(
                filtered_sin[:, first_wave : first_wave + wave_block],
                sine_part,
                CONTRACT_LAST,
                precision=PRECISE,
            )
        )
    potential = scale_long * potential
    pre_act = jnp.dot(
        message.astype(jnp.bfloat16), w_mix, preferred_element_type=jnp.float32
    ) + lax.dot_general(
        potential.astype(jnp.bfloat16), w_long, CONTRACT_FIRST, preferred_element_type=jnp.float32
    )
    refined = own_rows.astype(jnp.float32) + jax.nn.silu(pre_act)
    energy = living * jnp.sum(jax.nn.silu(refined) * w_energy[None, :], axis=1)
    grad_new = living[:, None] * w_energy[None, :] * silu_grad(refined)
    grad_pre = (grad_new * silu_grad(pre_act)).astype(jnp.bfloat16)
    adjoint = lax.dot_general(
        grad_pre, w_mix, CONTRACT_LAST, preferred_element_type=jnp.float32
    ).astype(jnp.bfloat16)
    pull_back = lax.dot_general(w_long, grad_pre, CONTRACT_LAST, preferred_element_type=jnp.float32)
    near_adjoint = extended(
        adjoint[None, None, None], (("gx", 0), ("gy", 1), ("gz", 2)), 1
    ).reshape(27, atom_count, channels)
    pull_c, pull_s = structure(pull_back, absolute, wave_vec, wave_block)
    back_c, back_s = lax.psum((pull_c, pull_s), ("gx", "gy", "gz"))

    def add_force(neighbour, near_force):
        others = lax.dynamic_index_in_dim(near_pos, neighbour, 0, keepdims=False)
        offset_vec, radial, radial_slope = pair_geometry(centre, others, neighbour)
        first_term = lax.dot_general(
            adjoint, fetch_basis(neighbour), CONTRACT_LAST, preferred_element_type=jnp.float32
        ).reshape(atom_count, basis_count, atom_count)
        near_rows = lax.dynamic_index_in_dim(near_adjoint, neighbour, 0, keepdims=False)
        second_term = jnp.einsum(
            "bic,jc->ibj", local_proj, near_rows, preferred_element_type=jnp.float32
        )
        strength = jnp.sum(radial_slope * (first_term + second_term), axis=1)
        return near_force + 2.0 / (CUTOFF * CUTOFF) * jnp.sum(
            strength[None, :, :] * offset_vec, axis=2
        )

    near_force = lax.fori_loop(0, 27, add_force, jnp.zeros((3, atom_count), jnp.float32))
    mixing = jnp.concatenate([pull_back, neutral], axis=0)
    weights_along = jnp.concatenate([filtered_sin, k_filter * back_s], axis=0)
    weights_across = jnp.concatenate([filtered_cos, k_filter * back_c], axis=0)
    ewald_grad = jnp.zeros((3, atom_count), jnp.float32)
    for first_wave in range(0, waves, wave_block):
        cosine, sine_part = phases(absolute, wave_vec, first_wave, wave_block)
        along_term = lax.dot_general(
            mixing,
            weights_along[:, first_wave : first_wave + wave_block],
            CONTRACT_FIRST,
            precision=PRECISE,
        )
        across_term = lax.dot_general(
            mixing,
            weights_across[:, first_wave : first_wave + wave_block],
            CONTRACT_FIRST,
            precision=PRECISE,
        )
        ewald_grad = ewald_grad + lax.dot_general(
            wave_vec[:, first_wave : first_wave + wave_block],
            cosine * along_term - sine_part * across_term,
            CONTRACT_LAST,
            precision=PRECISE,
        )
    forces = near_force - scale_long * ewald_grad
    return (
        refined.astype(jnp.bfloat16)[None, None, None],
        energy[None, None, None],
        forces[None, None, None],
    )


def solution(mesh):
    in_specs = (
        P("gx", "gy", "gz", None, None),
        P("gx", "gy", "gz", None, None),
        P("gx", "gy", "gz"),
        P(),
        P(),
        P(),
        P(),
        P(),
        P(),
        P(),
        P(),
    )
    out_specs = (
        P("gx", "gy", "gz", None, None),
        P("gx", "gy", "gz", None),
        P("gx", "gy", "gz", None, None),
    )
    return jax.shard_map(shards, mesh=mesh, in_specs=in_specs, out_specs=out_specs, check_vma=False)
```

profile of v0, /device:TPU:23, one launch (start us, length us, event | category | flops | bytes accessed | tf_op | source)
XLA Modules:
  0.0 663.8 jit_solution(11404104133226041706)
XLA Ops:
  7.2 6.4 collective-permute-start
  13.6 1.9 collective-permute-start.1
  17.1 6.6 collective-permute-start.7
  23.7 1.9 collective-permute-start.6
  27.7 1.2 fusion.69
  28.9 1.2 fusion.74
  30.2 1.2 fusion.81
  31.4 1.2 fusion.86
  32.7 1.2 fusion.93
  33.9 1.2 fusion.98
  35.2 1.2 fusion.106
  36.4 1.2 fusion.111
  39.9 98.9 %all-reduce = (f32[64]{0:T(128)S(1)}, f32[]{:T(128)}) all-reduce(f32[64]{0:T(128)S(1)} %get-tuple-element.752, f32[]{:T(128)} %fusion.291), channel_id=1, replica_groups=mesh['gx'=8,'gy'=8,'gz'=8] {'gx','gy','gz'}, use_global_device_ids=true, to_apply=%region_5.6 | all-reduce | flops 65 | bytes 520 | tf_op jit(solution)/shard_map/psum | solution.py:109
  139.5 2.1 collective-permute-start.3
  141.6 3.5 collective-permute-start.2
  145.2 1.9 collective-permute-start.9
  147.1 4.6 collective-permute-start.8
  151.7 1.9 collective-permute-start.5
  153.7 3.4 collective-permute-start.4
  157.1 2.8 collective-permute-start.11
  159.9 3.5 collective-permute-start.10
  163.6 2.9 collective-permute-done.11
  166.6 6.0 collective-permute-done.10
  173.3 20.3 %while.36 = (s32[]{:T(128)}, f32[128,128]{1,0:T(8,128)S(1)}, f32[27,3,128]{2,1,0:T(4,128)S(1)}, f32[1,1,1,3,128]{4,3,2,1,0:T(4,128)S(1)}, bf16[27,128,128]{2,1,0...) while((s32[]{:T(128)}, f32[128,128]{1,0:T(8,128)S(1)}, ...), condition=%wide.region_2.3_spmd.clone.clone, body=%wide.region_0.0_spmd.clone.clone.sunk | while | flops 34161064 | bytes 826287 | solution.py:142
  193.8 123.2 %all-reduce.8.cloned.1.call-done = (f32[65,2048]{1,0:T(8,128)}, f32[65,2048]{1,0:T(8,128)}) async-done(((f32[65,2048]{1,0:T(8,128)}, f32[65,2048]{1,0:T(8,128)}), (f32[65,2048]{1,0:T(8,128)}, f32[65,2048]{1,0:T(8,128)})) %all-reduce.8.cloned.1.call-update) | async-done | bytes 1064976 | tf_op jit(solution)/shard_map/psum | solution.py:109
  318.7 1.4 fusion.48
  320.1 1.3 fusion.104
  321.4 1.3 convolution_add_fusion.8
  322.7 1.3 convolution_add_fusion.7
  324.1 1.3 convolution_add_fusion.6
  325.4 1.3 convolution_add_fusion.5
  326.7 1.3 convolution_add_fusion.4
  328.0 1.3 convolution_add_fusion.3
  329.3 1.3 fusion.44
  331.6 1.9 collective-permute-start.13
  333.5 4.7 collective-permute-start.12
  338.4 1.2 fusion.71
  348.0 1.9 collective-permute-start.15
  349.9 3.4 collective-permute-start.14
  356.1 3.4 collective-permute-start.17
  359.5 2.1 collective-permute-start.16
  364.4 2.7 collective-permute-done.17
  367.0 6.8 %collective-permute-done.16 = bf16[3,3,1,128,128]{4,3,2,1,0:T(8,128)(2,1)} collective-permute-done((bf16[3,3,1,128,128]{4,3,2,1,0:T(8,128)(2,1)}, bf16[3,3,1,128,128]{4,3,2,1,0:T(8,128)(2,1)}, u32[]{:S(2)}, u32[]{:S(2)}) %collective-permute-start.16) | collective-permute-done | bytes 294944 | tf_op jit(solution)/shard_map/ppermute | solution.py:21
  373.8 2.0 pad_maximum_fusion.1
  375.8 67.3 %while.37 = (s32[]{:T(128)}, f32[3,128]{1,0:T(4,128)S(1)}, f32[27,3,128]{2,1,0:T(4,128)S(1)}, f32[1,1,1,3,128]{4,3,2,1,0:T(4,128)S(1)}, bf16[27,128,128]{2,1,0:T...) while((s32[]{:T(128)}, f32[3,128]{1,0:T(4,128)S(1)}, ...), condition=%wide.region_14.15_spmd.clone.clone, body=%wide.region_10.14_spmd.clone.clone.sunk | while | flops 51315852 | bytes 2604507 | solution.py:198
  443.1 199.9 %all-reduce.6.cloned.1.call-done = (f32[64,2048]{1,0:T(8,128)}, f32[64,2048]{1,0:T(8,128)}) async-done(((f32[64,2048]{1,0:T(8,128)}, f32[64,2048]{1,0:T(8,128)}), (f32[64,2048]{1,0:T(8,128)}, f32[64,2048]{1,0:T(8,128)})) %all-reduce.6.cloned.1.call-update) | async-done | bytes 1048592 | tf_op jit(solution)/shard_map/psum | solution.py:181
  643.0 1.3 fusion.293
  651.5 1.3 fusion.39
  (699 shorter events, 114.2 us)
Async XLA Ops:
  7.2 186.5 %copy-start = (bf16[128,128]{1,0:T(8,128)(2,1)S(1)}, bf16[128,128]{1,0:T(8,128)(2,1)}, u32[]{:S(2)}) copy-start(bf16[128,128]{1,0:T(8,128)(2,1)} %param.22) | copy-start | bytes 98308
  7.2 309.8 %all-reduce.8.cloned.1.call-start = ((), (), s32[]{:S(2)}) async-start(), calls=%async_computation.1 | async-start | bytes 2359296 | tf_op jit(solution)/shard_map/psum | solution.py:109
  7.2 132.2 %collective-permute-start = (f32[1,1,1,3,128]{4,2,3,1,0:T(1,128)}, f32[1,1,1,3,128]{4,2,3,1,0:T(1,128)S(1)}, u32[]{:S(2)}, u32[]{:S(2)}) collective-permute-start(f32[1,1,1,3,128]{4,2,3,1,0:T(1,128)} %param.19), channel_id=1, source_target_pairs={{0,64},{64,128},{128,192},{192,256},{256,320},{320,384},{384,448},... | collective-permute-start | bytes 4616 | tf_op jit(solution)/shard_map/ppermute | solution.py:21
  13.6 125.9 %collective-permute-start.1 = (f32[1,1,1,3,128]{4,2,3,1,0:T(1,128)}, f32[1,1,1,3,128]{4,2,3,1,0:T(1,128)S(1)}, u32[]{:S(2)}, u32[]{:S(2)}) collective-permute-start(f32[1,1,1,3,128]{4,2,3,1,0:T(1,128)} %param.19), channel_id=1, source_target_pairs={{64,0},{128,64},{192,128},{256,192},{320,256},{384,320},{448,384},... | collective-permute-start | bytes 4616 | tf_op jit(solution)/shard_map/ppermute | solution.py:22
  16.2 9.5 %copy-start.3 = (bf16[1,1,1,128,128]{4,3,2,1,0:T(8,128)(2,1)S(1)}, bf16[1,1,1,128,128]{4,3,2,1,0:T(8,128)(2,1)}, u32[]{:S(2)}) copy-start(bf16[1,1,1,128,128]{4,3,2,1,0:T(8,128)(2,1)} %param.18) | copy-start | bytes 98308
  17.1 8.7 %copy-start.7 = (s32[3,2048]{1,0:T(4,128)S(1)}, s32[3,2048]{1,0:T(4,128)}, u32[]{:S(2)}) copy-start(s32[3,2048]{1,0:T(4,128)} %param.28) | copy-start | bytes 73732
  17.1 128.0 %collective-permute-start.7 = (bf16[1,1,1,128,128]{4,3,2,1,0:T(8,128)(2,1)S(1)}, bf16[1,1,1,128,128]{4,3,2,1,0:T(8,128)(2,1)S(1)}, u32[]{:S(2)}, u32[]{:S(2)}) collective-permute-start(bf16[1,1,1,128,128]{4,3,2,1,0:T(8,128)(2,1)S(1)} %broadcast_multiply_fusion.2), channel_id=1, source_target_pairs={{64,0},{128,64},{192,128},{256,192},{320,256},{384,320},{448,384},... | collective-permute-start | bytes 98312 | tf_op jit(solution)/shard_map/ppermute | solution.py:22
  23.7 121.4 %collective-permute-start.6 = (bf16[1,1,1,128,128]{4,3,2,1,0:T(8,128)(2,1)S(1)}, bf16[1,1,1,128,128]{4,3,2,1,0:T(8,128)(2,1)S(1)}, u32[]{:S(2)}, u32[]{:S(2)}) collective-permute-start(bf16[1,1,1,128,128]{4,3,2,1,0:T(8,128)(2,1)S(1)} %broadcast_multiply_fusion.2), channel_id=1, source_target_pairs={{0,64},{64,128},{128,192},{192,256},{256,320},{320,384},{384,448},... | collective-permute-start | bytes 98312 | tf_op jit(solution)/shard_map/ppermute | solution.py:21
  25.9 316.2 %copy-start.26 = (f32[1,512]{1,0:T(1,128)}, f32[1,512]{1,0:T(1,128)S(1)}, u32[]{:S(2)}) copy-start(f32[1,512]{1,0:T(1,128)S(1)} %get-tuple-element.737) | copy-start | bytes 6148
  25.9 316.2 %copy-start.29 = (f32[1,512]{1,0:T(1,128)}, f32[1,512]{1,0:T(1,128)S(1)}, u32[]{:S(2)}) copy-start(f32[1,512]{1,0:T(1,128)S(1)} %get-tuple-element.747) | copy-start | bytes 6148
  25.9 316.2 %copy-start.32 = (f32[1,512]{1,0:T(1,128)}, f32[1,512]{1,0:T(1,128)S(1)}, u32[]{:S(2)}) copy-start(f32[1,512]{1,0:T(1,128)S(1)} %get-tuple-element.748) | copy-start | bytes 6148
  25.9 317.5 %copy-start.8 = (f32[1,512]{1,0:T(1,128)}, f32[1,512]{1,0:T(1,128)S(1)}, u32[]{:S(2)}) copy-start(f32[1,512]{1,0:T(1,128)S(1)} %get-tuple-element.738) | copy-start | bytes 6148
  25.9 317.5 %copy-start.10 = (f32[1,512]{1,0:T(1,128)}, f32[1,512]{1,0:T(1,128)S(1)}, u32[]{:S(2)}) copy-start(f32[1,512]{1,0:T(1,128)S(1)} %get-tuple-element.739) | copy-start | bytes 6148
  25.9 317.5 %copy-start.12 = (f32[1,512]{1,0:T(1,128)}, f32[1,512]{1,0:T(1,128)S(1)}, u32[]{:S(2)}) copy-start(f32[1,512]{1,0:T(1,128)S(1)} %get-tuple-element.740) | copy-start | bytes 6148
  25.9 318.7 %copy-start.14 = (f32[1,512]{1,0:T(1,128)}, f32[1,512]{1,0:T(1,128)S(1)}, u32[]{:S(2)}) copy-start(f32[1,512]{1,0:T(1,128)S(1)} %get-tuple-element.741) | copy-start | bytes 6148
  25.9 318.7 %copy-start.16 = (f32[1,512]{1,0:T(1,128)}, f32[1,512]{1,0:T(1,128)S(1)}, u32[]{:S(2)}) copy-start(f32[1,512]{1,0:T(1,128)S(1)} %get-tuple-element.742) | copy-start | bytes 6148
  25.9 318.7 %copy-start.18 = (f32[1,512]{1,0:T(1,128)}, f32[1,512]{1,0:T(1,128)S(1)}, u32[]{:S(2)}) copy-start(f32[1,512]{1,0:T(1,128)S(1)} %get-tuple-element.743) | copy-start | bytes 6148
  25.9 320.7 %copy-start.20 = (f32[1,512]{1,0:T(1,128)}, f32[1,512]{1,0:T(1,128)S(1)}, u32[]{:S(2)}) copy-start(f32[1,512]{1,0:T(1,128)S(1)} %get-tuple-element.744) | copy-start | bytes 6148
  26.0 320.7 %copy-start.22 = (f32[1,512]{1,0:T(1,128)}, f32[1,512]{1,0:T(1,128)S(1)}, u32[]{:S(2)}) copy-start(f32[1,512]{1,0:T(1,128)S(1)} %get-tuple-element.745) | copy-start | bytes 6148
  26.0 320.7 %copy-start.24 = (f32[1,512]{1,0:T(1,128)}, f32[1,512]{1,0:T(1,128)S(1)}, u32[]{:S(2)}) copy-start(f32[1,512]{1,0:T(1,128)S(1)} %get-tuple-element.746) | copy-start | bytes 6148
  26.8 326.5 %copy-start.5 = (f32[128]{0:T(128)}, f32[128]{0:T(128)S(1)}, u32[]{:S(2)}) copy-start(f32[128]{0:T(128)S(1)} %get-tuple-element.751) | copy-start | bytes 1540
  38.8 604.2 %all-reduce.6.cloned.1.call-start = ((), (), s32[]{:S(2)}) async-start(), calls=%async_computation | async-start | bytes 2097152 | tf_op jit(solution)/shard_map/psum | solution.py:181
  139.5 12.2 %collective-permute-start.3 = (f32[3,1,1,3,128]{4,2,3,1,0:T(1,128)S(1)}, f32[3,1,1,3,128]{4,2,3,1,0:T(1,128)S(1)}, u32[]{:S(2)}, u32[]{:S(2)}) collective-permute-start(f32[3,1,1,3,128]{4,2,3,1,0:T(1,128)S(1)} %constant_dynamic-update-slice_fusion), channel_id=1, source_target_pairs={{8,0},{16,8},{24,16},{32,24},{40,32},{48,40},{56,48},{0,56},{9,1},... | collective-permute-start | bytes 13832 | tf_op jit(solution)/shard_map/ppermute | solution.py:22
  141.6 10.1 %collective-permute-start.2 = (f32[3,1,1,3,128]{4,2,3,1,0:T(1,128)S(1)}, f32[3,1,1,3,128]{4,2,3,1,0:T(1,128)S(1)}, u32[]{:S(2)}, u32[]{:S(2)}) collective-permute-start(f32[3,1,1,3,128]{4,2,3,1,0:T(1,128)S(1)} %constant_dynamic-update-slice_fusion), channel_id=1, source_target_pairs={{0,8},{8,16},{16,24},{24,32},{32,40},{40,48},{48,56},{56,0},{1,9},... | collective-permute-start | bytes 13832 | tf_op jit(solution)/shard_map/ppermute | solution.py:21
  145.2 11.9 %collective-permute-start.9 = (bf16[3,1,1,128,128]{4,3,2,1,0:T(8,128)(2,1)S(1)}, bf16[3,1,1,128,128]{4,3,2,1,0:T(8,128)(2,1)S(1)}, u32[]{:S(2)}, u32[]{:S(2)}) collective-permute-start(bf16[3,1,1,128,128]{4,3,2,1,0:T(8,128)(2,1)S(1)} %pad_maximum_fusion.12), channel_id=1, source_target_pairs={{8,0},{16,8},{24,16},{32,24},{40,32},{48,40},{56,48},{0,56},{9,1},... | collective-permute-start | bytes 294920 | tf_op jit(solution)/shard_map/ppermute | solution.py:22
  147.1 9.9 %collective-permute-start.8 = (bf16[3,1,1,128,128]{4,3,2,1,0:T(8,128)(2,1)S(1)}, bf16[3,1,1,128,128]{4,3,2,1,0:T(8,128)(2,1)S(1)}, u32[]{:S(2)}, u32[]{:S(2)}) collective-permute-start(bf16[3,1,1,128,128]{4,3,2,1,0:T(8,128)(2,1)S(1)} %pad_maximum_fusion.12), channel_id=1, source_target_pairs={{0,8},{8,16},{16,24},{24,32},{32,40},{40,48},{48,56},{56,0},{1,9},... | collective-permute-start | bytes 294920 | tf_op jit(solution)/shard_map/ppermute | solution.py:21
  151.7 11.8 %collective-permute-start.5 = (f32[3,3,1,3,128]{4,2,3,1,0:T(1,128)S(1)}, f32[3,3,1,3,128]{4,2,3,1,0:T(1,128)S(1)}, u32[]{:S(2)}, u32[]{:S(2)}) collective-permute-start(f32[3,3,1,3,128]{4,2,3,1,0:T(1,128)S(1)} %pad_maximum_fusion.17), channel_id=1, source_target_pairs={{1,0},{2,1},{3,2},{4,3},{5,4},{6,5},{7,6},{0,7},{9,8},{10,9},{11,1... | collective-permute-start | bytes 41480 | tf_op jit(solution)/shard_map/ppermute | solution.py:22
  153.7 9.9 %collective-permute-start.4 = (f32[3,3,1,3,128]{4,2,3,1,0:T(1,128)S(1)}, f32[3,3,1,3,128]{4,2,3,1,0:T(1,128)S(1)}, u32[]{:S(2)}, u32[]{:S(2)}) collective-permute-start(f32[3,3,1,3,128]{4,2,3,1,0:T(1,128)S(1)} %pad_maximum_fusion.17), channel_id=1, source_target_pairs={{0,1},{1,2},{2,3},{3,4},{4,5},{5,6},{6,7},{7,0},{8,9},{9,10},{10,1... | collective-permute-start | bytes 41480 | tf_op jit(solution)/shard_map/ppermute | solution.py:21
  157.1 9.5 %collective-permute-start.11 = (bf16[3,3,1,128,128]{4,3,2,1,0:T(8,128)(2,1)S(1)}, bf16[3,3,1,128,128]{4,3,2,1,0:T(8,128)(2,1)S(1)}, u32[]{:S(2)}, u32[]{:S(2)}) collective-permute-start(bf16[3,3,1,128,128]{4,3,2,1,0:T(8,128)(2,1)S(1)} %pad_maximum_fusion.6), channel_id=1, source_target_pairs={{1,0},{2,1},{3,2},{4,3},{5,4},{6,5},{7,6},{0,7},{9,8},{10,9},{11,1... | collective-permute-start | bytes 884744 | tf_op jit(solution)/shard_map/ppermute | solution.py:22
  159.9 12.6 %collective-permute-start.10 = (bf16[3,3,1,128,128]{4,3,2,1,0:T(8,128)(2,1)S(1)}, bf16[3,3,1,128,128]{4,3,2,1,0:T(8,128)(2,1)S(1)}, u32[]{:S(2)}, u32[]{:S(2)}) collective-permute-start(bf16[3,3,1,128,128]{4,3,2,1,0:T(8,128)(2,1)S(1)} %pad_maximum_fusion.6), channel_id=1, source_target_pairs={{0,1},{1,2},{2,3},{3,4},{4,5},{5,6},{6,7},{7,0},{8,9},{9,10},{10,1... | collective-permute-start | bytes 884744 | tf_op jit(solution)/shard_map/ppermute | solution.py:21
  173.3 145.4 %copy-start.2 = (f32[64,2048]{1,0:T(8,128)S(1)}, f32[64,2048]{1,0:T(8,128)}, u32[]{:S(2)}) copy-start(f32[64,2048]{1,0:T(8,128)} %param.27) | copy-start | bytes 1572868
  329.3 1.3 copy-start.35
  329.3 1.3 copy-start.39
  331.6 16.3 %collective-permute-start.13 = (bf16[1,1,1,128,128]{4,3,2,1,0:T(8,128)(2,1)S(1)}, bf16[1,1,1,128,128]{4,3,2,1,0:T(8,128)(2,1)S(1)}, u32[]{:S(2)}, u32[]{:S(2)}) collective-permute-start(bf16[1,1,1,128,128]{4,3,2,1,0:T(8,128)(2,1)S(1)} %bitcast.201), channel_id=1, source_target_pairs={{64,0},{128,64},{192,128},{256,192},{320,256},{384,320},{448,384},... | collective-permute-start | bytes 98312 | tf_op jit(solution)/shard_map/ppermute | solution.py:22
  333.5 14.4 %collective-permute-start.12 = (bf16[1,1,1,128,128]{4,3,2,1,0:T(8,128)(2,1)S(1)}, bf16[1,1,1,128,128]{4,3,2,1,0:T(8,128)(2,1)S(1)}, u32[]{:S(2)}, u32[]{:S(2)}) collective-permute-start(bf16[1,1,1,128,128]{4,3,2,1,0:T(8,128)(2,1)S(1)} %bitcast.202), channel_id=1, source_target_pairs={{0,64},{64,128},{128,192},{192,256},{256,320},{320,384},{384,448},... | collective-permute-start | bytes 98312 | tf_op jit(solution)/shard_map/ppermute | solution.py:21
  347.9 5.4 copy-start.27
  347.9 5.4 copy-start.30
  347.9 5.4 copy-start.33
  348.0 6.6 collective-permute-start.15
  349.9 5.4 collective-permute-start.14
  356.1 11.0 %collective-permute-start.17 = (bf16[3,3,1,128,128]{4,3,2,1,0:T(8,128)(2,1)}, bf16[3,3,1,128,128]{4,3,2,1,0:T(8,128)(2,1)S(1)}, u32[]{:S(2)}, u32[]{:S(2)}) collective-permute-start(bf16[3,3,1,128,128]{4,3,2,1,0:T(8,128)(2,1)} %pad_maximum_fusion.7), channel_id=1, source_target_pairs={{1,0},{2,1},{3,2},{4,3},{5,4},{6,5},{7,6},{0,7},{9,8},{10,9},{11,1... | collective-permute-start | bytes 884744 | tf_op jit(solution)/shard_map/ppermute | solution.py:22
  359.5 14.3 %collective-permute-start.16 = (bf16[3,3,1,128,128]{4,3,2,1,0:T(8,128)(2,1)}, bf16[3,3,1,128,128]{4,3,2,1,0:T(8,128)(2,1)}, u32[]{:S(2)}, u32[]{:S(2)}) collective-permute-start(bf16[3,3,1,128,128]{4,3,2,1,0:T(8,128)(2,1)} %pad_maximum_fusion.7), channel_id=1, source_target_pairs={{0,1},{1,2},{2,3},{3,4},{4,5},{5,6},{6,7},{7,0},{8,9},{9,10},{10,1... | collective-permute-start | bytes 884744 | tf_op jit(solution)/shard_map/ppermute | solution.py:21
  643.0 1.3 copy-start.31
  643.0 1.3 copy-start.34
  646.2 1.2 copy-start.15
  646.2 1.2 copy-start.17
  646.2 1.2 copy-start.19
  647.5 1.2 copy-start.9
  (13 other events, 11.9 us)
Sparse Core Ops, SparseCore 0:
  38.9 278.0 all-reduce.7
  363.3 279.6 all-reduce.5
where the time goes:
time: 675 us; the launch traced here: 664 us
  waiting for transfers between devices  342 us (51%)
  blocking collectives  98.9 us (15%)
  matrix products  87.7 us (13%)
  starting transfers between devices  58.1 us (9%)
  other arithmetic  34.2 us (5%)
  local copies, waits for them, and re-layouts  18.9 us (3%)
  between operations  16.1 us (2%)
  loops' own time  7.66 us (1%)
    psum x1, waiting for transfers between devices, shards(): back_c, back_s = lax.psum((pull_c, pull_s), ('gx', 'gy', 'gz'))  200 us
    psum x1, waiting for transfers between devices, shards(): lax.psum((local_c, local_s, jnp.sum(charges, axis=1), jnp.sum(living)), (...  123 us
    psum x1, blocking collectives, shards(): lax.psum((local_c, local_s, jnp.sum(charges, axis=1), jnp.sum(living)), (...  98.9 us
    ppermute x9, starting transfers between devices, extended(): before = lax.ppermute(last, axis, up)  33.5 us
    dot_general x27, matrix products, add_force(): jnp.einsum('bic,jc->ibj', local_proj, near_rows, preferred_element_type=j...  26 us
    ppermute x9, starting transfers between devices, extended(): after = lax.ppermute(initial, axis, down)  24.6 us
    ppermute x9, waiting for transfers between devices, extended(): before = lax.ppermute(last, axis, up)  13.5 us
  transfers between devices with their start and end apart: 20, of which 7 were waited for; matrix products, arithmetic and copies ran while one was open for 16% of the time, Pallas kernels for 0%

commit v1 on v0

--- a/solution.py
+++ b/solution.py
@@ -178,7 +178,7 @@
         adjoint[None, None, None], (("gx", 0), ("gy", 1), ("gz", 2)), 1
     ).reshape(27, atom_count, channels)
     pull_c, pull_s = structure(pull_back, absolute, wave_vec, wave_block)
-    back_c, back_s = lax.psum((pull_c, pull_s), ("gx", "gy", "gz"))
+    back_c, back_s = lax.psum(lax.psum((pull_c, pull_s), "gx"), ("gy", "gz"))
 
     def add_force(neighbour, near_force):
         others = lax.dynamic_index_in_dim(near_pos, neighbour, 0, keepdims=False)

time: 675 us -> 1080 us (1.60)
  the two profiles are of different devices: /device:TPU:23 before, /device:TPU:2 now
where the time goes in v1:
time: 1080 us; the launch traced here: 1070 us
  waiting for transfers between devices  744 us (69%)
  blocking collectives  102 us (9%)
  matrix products  88.2 us (8%)
  starting transfers between devices  61.5 us (6%)
  other arithmetic  34.2 us (3%)
  local copies, waits for them, and re-layouts  19.5 us (2%)
  between operations  15.8 us (1%)
    psum x2, waiting for transfers between devices, shards(): back_c, back_s = lax.psum(lax.psum((pull_c, pull_s), 'gx'), ('gy', 'gz'))  597 us
    psum x1, waiting for transfers between devices, shards(): lax.psum((local_c, local_s, jnp.sum(charges, axis=1), jnp.sum(living)), (...  119 us
    psum x1, blocking collectives, shards(): lax.psum((local_c, local_s, jnp.sum(charges, axis=1), jnp.sum(living)), (...  102 us
    ppermute x9, starting transfers between devices, extended(): after = lax.ppermute(initial, axis, down)  38.7 us
    dot_general x27, matrix products, add_force(): jnp.einsum('bic,jc->ibj', local_proj, near_rows, preferred_element_type=j...  26 us
    ppermute x9, starting transfers between devices, extended(): before = lax.ppermute(last, axis, up)  22.6 us
  transfers between devices with their start and end apart: 21, of which 9 were waited for; matrix products, arithmetic and copies ran while one was open for 10% of the time, Pallas kernels for 0%

profile of v1, /device:TPU:2, one launch (start us, length us, event | category | flops | bytes accessed | tf_op | source)
XLA Modules:
  0.0 1072.3 jit_solution(4137378348182602672)
XLA Ops:
  7.2 1.9 collective-permute-start
  9.2 10.4 collective-permute-start.1
  21.1 2.6 collective-permute-start.7
  23.7 1.9 collective-permute-start.6
  27.7 1.2 fusion.69
  28.9 1.3 fusion.74
  31.4 1.2 fusion.86
  33.9 1.2 fusion.98
  36.4 1.2 fusion.111
  39.5 101.5 %all-reduce = (f32[64]{0:T(128)S(1)}, f32[]{:T(128)}) all-reduce(f32[64]{0:T(128)S(1)} %get-tuple-element.754, f32[]{:T(128)} %fusion.291), channel_id=1, replica_groups=mesh['gx'=8,'gy'=8,'gz'=8] {'gx','gy','gz'}, use_global_device_ids=true, to_apply=%region_5.6 | all-reduce | flops 65 | bytes 520 | tf_op jit(solution)/shard_map/psum | solution.py:109
  141.1 2.4 collective-permute-start.3
  143.5 3.4 collective-permute-start.2
  147.0 3.6 collective-permute-start.9
  150.6 2.2 collective-permute-start.8
  152.9 4.4 collective-permute-start.5
  157.3 1.9 collective-permute-start.4
  159.2 4.8 collective-permute-start.11
  164.1 2.4 collective-permute-start.10
  167.3 4.4 collective-permute-done.11
  171.6 4.5 collective-permute-done.10
  176.9 20.3 %while.36 = (s32[]{:T(128)}, f32[128,128]{1,0:T(8,128)S(1)}, f32[27,3,128]{2,1,0:T(4,128)S(1)}, f32[1,1,1,3,128]{4,3,2,1,0:T(4,128)S(1)}, bf16[27,128,128]{2,1,0...) while((s32[]{:T(128)}, f32[128,128]{1,0:T(8,128)S(1)}, ...), condition=%wide.region_2.3_spmd.clone.clone, body=%wide.region_0.0_spmd.clone.clone.sunk | while | flops 34161064 | bytes 826287 | solution.py:142
  197.4 118.6 %all-reduce.8.cloned.1.call-done = (f32[65,2048]{1,0:T(8,128)}, f32[65,2048]{1,0:T(8,128)}) async-done(((f32[65,2048]{1,0:T(8,128)}, f32[65,2048]{1,0:T(8,128)}), (f32[65,2048]{1,0:T(8,128)}, f32[65,2048]{1,0:T(8,128)})) %all-reduce.8.cloned.1.call-update) | async-done | bytes 1064976 | tf_op jit(solution)/shard_map/psum | solution.py:109
  317.6 1.4 fusion.48
  319.0 1.3 fusion.104
  320.3 1.3 convolution_add_fusion.8
  321.7 1.3 convolution_add_fusion.7
  323.0 1.3 convolution_add_fusion.6
  324.3 1.3 convolution_add_fusion.5
  325.6 1.3 convolution_add_fusion.4
  326.9 1.3 convolution_add_fusion.3
  328.2 1.3 fusion.44
  329.6 1.4 multiply_convert_fusion.2
  331.1 5.4 collective-permute-start.13
  336.5 2.1 collective-permute-start.12
  350.5 2.4 collective-permute-start.15
  352.9 3.4 collective-permute-start.14
  357.0 4.3 collective-permute-done.14
  362.0 2.7 collective-permute-start.17
  364.7 3.3 collective-permute-start.16
  368.1 1.5 copy.38
  370.8 6.2 collective-permute-done.17
  376.9 8.4 collective-permute-done.16
  385.4 2.0 pad_maximum_fusion.1
  387.4 44.9 %all-reduce.12.cloned.1.call-done = (f32[64,2048]{1,0:T(8,128)}, f32[64,2048]{1,0:T(8,128)}) async-done(((f32[64,2048]{1,0:T(8,128)}, f32[64,2048]{1,0:T(8,128)}), (f32[64,2048]{1,0:T(8,128)}, f32[64,2048]{1,0:T(8,128)})) %all-reduce.12.cloned.1.call-update) | async-done | bytes 1048592 | tf_op jit(solution)/shard_map/psum | solution.py:181
  432.3 67.3 %while.37 = (s32[]{:T(128)}, f32[3,128]{1,0:T(4,128)S(1)}, f32[27,3,128]{2,1,0:T(4,128)S(1)}, f32[1,1,1,3,128]{4,3,2,1,0:T(4,128)S(1)}, bf16[27,128,128]{2,1,0:T...) while((s32[]{:T(128)}, f32[3,128]{1,0:T(4,128)S(1)}, ...), condition=%wide.region_14.15_spmd.clone.clone, body=%wide.region_10.14_spmd.clone.clone.sunk | while | flops 51315852 | bytes 2604507 | solution.py:198
  499.6 552.2 %all-reduce.10.cloned.1.call-done = (f32[64,2048]{1,0:T(8,128)}, f32[64,2048]{1,0:T(8,128)}) async-done(((f32[64,2048]{1,0:T(8,128)}, f32[64,2048]{1,0:T(8,128)}), (f32[64,2048]{1,0:T(8,128)}, f32[64,2048]{1,0:T(8,128)})) %all-reduce.10.cloned.1.call-update) | async-done | bytes 1048592 | tf_op jit(solution)/shard_map/psum | solution.py:181
  1051.8 1.3 fusion.293
  1060.3 1.3 fusion.39
  (708 shorter events, 117.1 us)
Async XLA Ops:
  7.2 190.0 %copy-start = (bf16[128,128]{1,0:T(8,128)(2,1)S(1)}, bf16[128,128]{1,0:T(8,128)(2,1)}, u32[]{:S(2)}) copy-start(bf16[128,128]{1,0:T(8,128)(2,1)} %param.22) | copy-start | bytes 98308
  7.2 308.7 %all-reduce.8.cloned.1.call-start = ((), (), s32[]{:S(2)}) async-start(), calls=%async_computation | async-start | bytes 2359296 | tf_op jit(solution)/shard_map/psum | solution.py:109
  7.2 133.8 %collective-permute-start = (f32[1,1,1,3,128]{4,2,3,1,0:T(1,128)}, f32[1,1,1,3,128]{4,2,3,1,0:T(1,128)S(1)}, u32[]{:S(2)}, u32[]{:S(2)}) collective-permute-start(f32[1,1,1,3,128]{4,2,3,1,0:T(1,128)} %param.19), channel_id=1, source_target_pairs={{0,64},{64,128},{128,192},{192,256},{256,320},{320,384},{384,448},... | collective-permute-start | bytes 4616 | tf_op jit(solution)/shard_map/ppermute | solution.py:21
  9.2 131.9 %collective-permute-start.1 = (f32[1,1,1,3,128]{4,2,3,1,0:T(1,128)}, f32[1,1,1,3,128]{4,2,3,1,0:T(1,128)S(1)}, u32[]{:S(2)}, u32[]{:S(2)}) collective-permute-start(f32[1,1,1,3,128]{4,2,3,1,0:T(1,128)} %param.19), channel_id=1, source_target_pairs={{64,0},{128,64},{192,128},{256,192},{320,256},{384,320},{448,384},... | collective-permute-start | bytes 4616 | tf_op jit(solution)/shard_map/ppermute | solution.py:22
  20.2 6.6 copy-start.34
  20.2 5.5 copy-start.3
  21.1 4.7 copy-start.7
  21.1 125.8 %collective-permute-start.7 = (bf16[1,1,1,128,128]{4,3,2,1,0:T(8,128)(2,1)S(1)}, bf16[1,1,1,128,128]{4,3,2,1,0:T(8,128)(2,1)S(1)}, u32[]{:S(2)}, u32[]{:S(2)}) collective-permute-start(bf16[1,1,1,128,128]{4,3,2,1,0:T(8,128)(2,1)S(1)} %broadcast_multiply_fusion.2), channel_id=1, source_target_pairs={{64,0},{128,64},{192,128},{256,192},{320,256},{384,320},{448,384},... | collective-permute-start | bytes 98312 | tf_op jit(solution)/shard_map/ppermute | solution.py:22
  23.7 123.2 %collective-permute-start.6 = (bf16[1,1,1,128,128]{4,3,2,1,0:T(8,128)(2,1)S(1)}, bf16[1,1,1,128,128]{4,3,2,1,0:T(8,128)(2,1)S(1)}, u32[]{:S(2)}, u32[]{:S(2)}) collective-permute-start(bf16[1,1,1,128,128]{4,3,2,1,0:T(8,128)(2,1)S(1)} %broadcast_multiply_fusion.2), channel_id=1, source_target_pairs={{0,64},{64,128},{128,192},{192,256},{256,320},{320,384},{384,448},... | collective-permute-start | bytes 98312 | tf_op jit(solution)/shard_map/ppermute | solution.py:21
  25.8 303.7 %copy-start.38 = (f32[128]{0:T(128)}, f32[128]{0:T(128)S(1)}, u32[]{:S(2)}) copy-start(f32[128]{0:T(128)S(1)} %compare_convert_fusion.1) | copy-start | bytes 1540
  25.9 317.8 %copy-start.8 = (f32[1,512]{1,0:T(1,128)}, f32[1,512]{1,0:T(1,128)S(1)}, u32[]{:S(2)}) copy-start(f32[1,512]{1,0:T(1,128)S(1)} %get-tuple-element.740) | copy-start | bytes 6148
  25.9 317.8 %copy-start.10 = (f32[1,512]{1,0:T(1,128)}, f32[1,512]{1,0:T(1,128)S(1)}, u32[]{:S(2)}) copy-start(f32[1,512]{1,0:T(1,128)S(1)} %get-tuple-element.741) | copy-start | bytes 6148
  25.9 317.8 %copy-start.12 = (f32[1,512]{1,0:T(1,128)}, f32[1,512]{1,0:T(1,128)S(1)}, u32[]{:S(2)}) copy-start(f32[1,512]{1,0:T(1,128)S(1)} %get-tuple-element.742) | copy-start | bytes 6148
  25.9 319.0 %copy-start.14 = (f32[1,512]{1,0:T(1,128)}, f32[1,512]{1,0:T(1,128)S(1)}, u32[]{:S(2)}) copy-start(f32[1,512]{1,0:T(1,128)S(1)} %get-tuple-element.743) | copy-start | bytes 6148
  25.9 319.0 %copy-start.16 = (f32[1,512]{1,0:T(1,128)}, f32[1,512]{1,0:T(1,128)S(1)}, u32[]{:S(2)}) copy-start(f32[1,512]{1,0:T(1,128)S(1)} %get-tuple-element.744) | copy-start | bytes 6148
  25.9 319.0 %copy-start.18 = (f32[1,512]{1,0:T(1,128)}, f32[1,512]{1,0:T(1,128)S(1)}, u32[]{:S(2)}) copy-start(f32[1,512]{1,0:T(1,128)S(1)} %get-tuple-element.745) | copy-start | bytes 6148
  25.9 320.2 %copy-start.20 = (f32[1,512]{1,0:T(1,128)}, f32[1,512]{1,0:T(1,128)S(1)}, u32[]{:S(2)}) copy-start(f32[1,512]{1,0:T(1,128)S(1)} %get-tuple-element.746) | copy-start | bytes 6148
  25.9 320.2 %copy-start.22 = (f32[1,512]{1,0:T(1,128)}, f32[1,512]{1,0:T(1,128)S(1)}, u32[]{:S(2)}) copy-start(f32[1,512]{1,0:T(1,128)S(1)} %get-tuple-element.747) | copy-start | bytes 6148
  26.0 320.2 %copy-start.24 = (f32[1,512]{1,0:T(1,128)}, f32[1,512]{1,0:T(1,128)S(1)}, u32[]{:S(2)}) copy-start(f32[1,512]{1,0:T(1,128)S(1)} %get-tuple-element.748) | copy-start | bytes 6148
  26.0 321.4 %copy-start.26 = (f32[1,512]{1,0:T(1,128)}, f32[1,512]{1,0:T(1,128)S(1)}, u32[]{:S(2)}) copy-start(f32[1,512]{1,0:T(1,128)S(1)} %get-tuple-element.739) | copy-start | bytes 6148
  26.0 321.4 %copy-start.28 = (f32[1,512]{1,0:T(1,128)}, f32[1,512]{1,0:T(1,128)S(1)}, u32[]{:S(2)}) copy-start(f32[1,512]{1,0:T(1,128)S(1)} %get-tuple-element.749) | copy-start | bytes 6148
  26.0 321.4 %copy-start.30 = (f32[1,512]{1,0:T(1,128)}, f32[1,512]{1,0:T(1,128)S(1)}, u32[]{:S(2)}) copy-start(f32[1,512]{1,0:T(1,128)S(1)} %get-tuple-element.750) | copy-start | bytes 6148
  26.8 320.7 %copy-start.5 = (f32[128]{0:T(128)}, f32[128]{0:T(128)S(1)}, u32[]{:S(2)}) copy-start(f32[128]{0:T(128)S(1)} %get-tuple-element.753) | copy-start | bytes 1540
  38.8 393.5 %all-reduce.12.cloned.1.call-start = ((), (), s32[]{:S(2)}) async-start(), calls=%async_computation.2 | async-start | bytes 2097152 | tf_op jit(solution)/shard_map/psum | solution.py:181
  141.1 11.8 %collective-permute-start.3 = (f32[3,1,1,3,128]{4,2,3,1,0:T(1,128)S(1)}, f32[3,1,1,3,128]{4,2,3,1,0:T(1,128)S(1)}, u32[]{:S(2)}, u32[]{:S(2)}) collective-permute-start(f32[3,1,1,3,128]{4,2,3,1,0:T(1,128)S(1)} %constant_dynamic-update-slice_fusion), channel_id=1, source_target_pairs={{8,0},{16,8},{24,16},{32,24},{40,32},{48,40},{56,48},{0,56},{9,1},... | collective-permute-start | bytes 13832 | tf_op jit(solution)/shard_map/ppermute | solution.py:22
  143.5 9.3 collective-permute-start.2
  147.0 12.2 %collective-permute-start.9 = (bf16[3,1,1,128,128]{4,3,2,1,0:T(8,128)(2,1)S(1)}, bf16[3,1,1,128,128]{4,3,2,1,0:T(8,128)(2,1)S(1)}, u32[]{:S(2)}, u32[]{:S(2)}) collective-permute-start(bf16[3,1,1,128,128]{4,3,2,1,0:T(8,128)(2,1)S(1)} %pad_maximum_fusion.12), channel_id=1, source_target_pairs={{8,0},{16,8},{24,16},{32,24},{40,32},{48,40},{56,48},{0,56},{9,1},... | collective-permute-start | bytes 294920 | tf_op jit(solution)/shard_map/ppermute | solution.py:22
  150.6 8.6 collective-permute-start.8
  152.9 14.3 %collective-permute-start.5 = (f32[3,3,1,3,128]{4,2,3,1,0:T(1,128)S(1)}, f32[3,3,1,3,128]{4,2,3,1,0:T(1,128)S(1)}, u32[]{:S(2)}, u32[]{:S(2)}) collective-permute-start(f32[3,3,1,3,128]{4,2,3,1,0:T(1,128)S(1)} %pad_maximum_fusion.17), channel_id=1, source_target_pairs={{1,0},{2,1},{3,2},{4,3},{5,4},{6,5},{7,6},{0,7},{9,8},{10,9},{11,1... | collective-permute-start | bytes 41480 | tf_op jit(solution)/shard_map/ppermute | solution.py:22
  157.3 9.9 collective-permute-start.4
  159.2 12.4 %collective-permute-start.11 = (bf16[3,3,1,128,128]{4,3,2,1,0:T(8,128)(2,1)S(1)}, bf16[3,3,1,128,128]{4,3,2,1,0:T(8,128)(2,1)S(1)}, u32[]{:S(2)}, u32[]{:S(2)}) collective-permute-start(bf16[3,3,1,128,128]{4,3,2,1,0:T(8,128)(2,1)S(1)} %pad_maximum_fusion.6), channel_id=1, source_target_pairs={{1,0},{2,1},{3,2},{4,3},{5,4},{6,5},{7,6},{0,7},{9,8},{10,9},{11,1... | collective-permute-start | bytes 884744 | tf_op jit(solution)/shard_map/ppermute | solution.py:22
  164.1 12.0 %collective-permute-start.10 = (bf16[3,3,1,128,128]{4,3,2,1,0:T(8,128)(2,1)S(1)}, bf16[3,3,1,128,128]{4,3,2,1,0:T(8,128)(2,1)S(1)}, u32[]{:S(2)}, u32[]{:S(2)}) collective-permute-start(bf16[3,3,1,128,128]{4,3,2,1,0:T(8,128)(2,1)S(1)} %pad_maximum_fusion.6), channel_id=1, source_target_pairs={{0,1},{1,2},{2,3},{3,4},{4,5},{5,6},{6,7},{7,0},{8,9},{9,10},{10,1... | collective-permute-start | bytes 884744 | tf_op jit(solution)/shard_map/ppermute | solution.py:21
  167.1 150.5 %copy-start.36 = (f32[64]{0:T(128)}, f32[64]{0:T(128)S(1)}, u32[]{:S(2)}) copy-start(f32[64]{0:T(128)S(1)} %broadcast_divide_fusion) | copy-start | bytes 772
  167.3 9.0 copy-start.1
  176.9 140.8 %copy-start.2 = (f32[64,2048]{1,0:T(8,128)S(1)}, f32[64,2048]{1,0:T(8,128)}, u32[]{:S(2)}) copy-start(f32[64,2048]{1,0:T(8,128)} %param.27) | copy-start | bytes 1572868
  328.2 1.3 copy-start.32
  328.2 1.3 copy-start.42
  331.1 19.3 %collective-permute-start.13 = (bf16[1,1,1,128,128]{4,3,2,1,0:T(8,128)(2,1)S(1)}, bf16[1,1,1,128,128]{4,3,2,1,0:T(8,128)(2,1)S(1)}, u32[]{:S(2)}, u32[]{:S(2)}) collective-permute-start(bf16[1,1,1,128,128]{4,3,2,1,0:T(8,128)(2,1)S(1)} %bitcast.201), channel_id=1, source_target_pairs={{64,0},{128,64},{192,128},{256,192},{320,256},{384,320},{448,384},... | collective-permute-start | bytes 98312 | tf_op jit(solution)/shard_map/ppermute | solution.py:22
  336.5 13.9 %collective-permute-start.12 = (bf16[1,1,1,128,128]{4,3,2,1,0:T(8,128)(2,1)S(1)}, bf16[1,1,1,128,128]{4,3,2,1,0:T(8,128)(2,1)S(1)}, u32[]{:S(2)}, u32[]{:S(2)}) collective-permute-start(bf16[1,1,1,128,128]{4,3,2,1,0:T(8,128)(2,1)S(1)} %bitcast.202), channel_id=1, source_target_pairs={{0,64},{64,128},{128,192},{192,256},{256,320},{320,384},{384,448},... | collective-permute-start | bytes 98312 | tf_op jit(solution)/shard_map/ppermute | solution.py:21
  350.4 6.0 copy-start.35
  350.4 701.4 %all-reduce.10.cloned.1.call-start = ((), (), s32[]{:S(2)}) async-start(), calls=%async_computation.1 | async-start | bytes 2097152 | tf_op jit(solution)/shard_map/psum | solution.py:181
  350.5 6.5 collective-permute-start.15
  352.9 8.3 collective-permute-start.14
  356.6 11.5 %copy-start.37 = (f32[64]{0:T(128)S(1)}, f32[64]{0:T(128)}, u32[]{:S(2)}) copy-start(f32[64]{0:T(128)} %copy-done.36) | copy-start | bytes 772
  356.6 11.5 %copy-start.39 = (f32[128]{0:T(128)S(1)}, f32[128]{0:T(128)}, u32[]{:S(2)}) copy-start(f32[128]{0:T(128)} %copy-done.38) | copy-start | bytes 1540
  362.0 15.0 %collective-permute-start.17 = (bf16[3,3,1,128,128]{4,3,2,1,0:T(8,128)(2,1)}, bf16[3,3,1,128,128]{4,3,2,1,0:T(8,128)(2,1)S(1)}, u32[]{:S(2)}, u32[]{:S(2)}) collective-permute-start(bf16[3,3,1,128,128]{4,3,2,1,0:T(8,128)(2,1)} %pad_maximum_fusion.7), channel_id=1, source_target_pairs={{1,0},{2,1},{3,2},{4,3},{5,4},{6,5},{7,6},{0,7},{9,8},{10,9},{11,1... | collective-permute-start | bytes 884744 | tf_op jit(solution)/shard_map/ppermute | solution.py:22
  364.7 20.7 %collective-permute-start.16 = (bf16[3,3,1,128,128]{4,3,2,1,0:T(8,128)(2,1)}, bf16[3,3,1,128,128]{4,3,2,1,0:T(8,128)(2,1)}, u32[]{:S(2)}, u32[]{:S(2)}) collective-permute-start(bf16[3,3,1,128,128]{4,3,2,1,0:T(8,128)(2,1)} %pad_maximum_fusion.7), channel_id=1, source_target_pairs={{0,1},{1,2},{2,3},{3,4},{4,5},{5,6},{6,7},{7,0},{8,9},{9,10},{10,1... | collective-permute-start | bytes 884744 | tf_op jit(solution)/shard_map/ppermute | solution.py:21
  1051.8 1.3 copy-start.31
  (17 other events, 17.3 us)
Sparse Core Ops, SparseCore 0:
  39.0 276.9 all-reduce.7
  350.5 81.7 all-reduce.11
  435.2 616.5 all-reduce.9
